TPU v7x, 128 devices: a whole 4x4x4 slice. The times are simulated.
128 devices in a mesh: dp: 8 (over z, x_hi), tensor: 16 (over y, x_lo, core).
Axes of the slice: x: 4 (x_hi: 2, x_lo: 2; x = x_hi * 2 + x_lo), y: 4, z: 4, core: 2. Of those that a mesh axis runs over, the one named last changes fastest.
Arguments:
- tokens: bfloat16 [4096, 8192], P('dp', 'tensor'), may hold values from -6 to 6
- frozen: bfloat16 [8192, 8192], P('tensor'), may hold values from -0.0625 to 0.0625
- local_param: float32 [64, 128, 128], P('tensor'), may hold values from -0.2 to 0.2
- cross_param: float32 [4, 64, 128, 128], P(None, 'tensor'), may hold values from -0.2 to 0.2
- out_grad: bfloat16 [4096, 8192], P('dp', 'tensor'), may hold values from -0.09375 to 0.09375
Outputs:
- output: float32 [4096, 8192], P('dp', 'tensor')
- local_grad: float32 [64, 128, 128], P('tensor')
- cross_grad: float32 [4, 64, 128, 128], P(None, 'tensor')
All inputs are finite; a program needn't handle non-finite values.
Results may differ from a plain program's by a relative error of at most 0.0029.
Values may be sent and summed in bfloat16 or wider, within the bound.
A program may use at most 192 MiB of HBM per device.

v0:
```python
import jax
import jax.numpy as jnp
from jax import lax
from jax.sharding import PartitionSpec as P


def from_partner(shard, axis, stride):
    return lax.ppermute(shard, axis, [(i, i ^ 1 << stride) for i in range(lax.axis_size(axis))])


def cayley_block(param):
    highest = lax.Precision.HIGHEST
    skew = param - param.T
    identity = jnp.eye(param.shape[0], dtype=param.dtype)
    one_minus = identity - skew
    spd_matrix = identity - jnp.dot(skew, skew, precision=highest)
    numerator = jnp.dot(one_minus, one_minus, precision=highest)
    chol_factor = jnp.linalg.cholesky(spd_matrix)
    return jax.scipy.linalg.cho_solve((chol_factor, True), numerator.T).T


def cayley_many(params):
    return jax.vmap(cayley_block)(params)


def cayley_pull(param, matrix_grad):
    unused, pullback = jax.vjp(cayley_many, param)
    return pullback(matrix_grad)[0]


def split_halves(state, upper_side, blocks_dev, half_block):
    halves = state.reshape(state.shape[0], 2, blocks_dev, half_block)
    own_part = jnp.where(upper_side, halves[:, 1], halves[:, 0])
    other_part = jnp.where(upper_side, halves[:, 0], halves[:, 1])
    return (own_part, other_part)


def join_pair(own_part, received, upper_side):
    low_half = jnp.where(upper_side, received, own_part)
    high_half = jnp.where(upper_side, own_part, received)
    return jnp.concatenate([low_half, high_half], axis=-1)


def split_pair(vector, upper_side, half_block):
    low_half = vector[..., :half_block]
    high_half = vector[..., half_block:]
    keep_part = jnp.where(upper_side, high_half, low_half)
    give_part = jnp.where(upper_side, low_half, high_half)
    return (keep_part, give_part)


def merge_halves(keep_part, returned, upper_side):
    first_half = jnp.where(upper_side, returned, keep_part)
    second_half = jnp.where(upper_side, keep_part, returned)
    return jnp.stack([first_half, second_half], axis=1).reshape(keep_part.shape[0], -1)


def sum_data(value):
    return lax.psum(value, "dp")


def body(tokens, frozen, local_param, cross_param, out_grad):
    highest = lax.Precision.HIGHEST
    token_count, rows_dev = tokens.shape
    block = local_param.shape[-1]
    half_block = block // 2
    blocks_dev = local_param.shape[0]
    levels = lax.axis_size("tensor").bit_length() - 1
    position = lax.axis_index("tensor")
    local_rot = cayley_many(local_param)
    cross_rot = [cayley_many(cross_param[level_idx]) for level_idx in range(levels)]
    inputs = tokens.astype(jnp.float32).reshape(token_count, blocks_dev, block)
    state = jnp.einsum("tci,cij->tcj", inputs, local_rot, precision=highest).reshape(
        token_count, rows_dev
    )
    saved = []
    for level_idx in range(levels):
        upper_side = position >> level_idx & 1 == 1
        own_part, other_part = split_halves(state, upper_side, blocks_dev, half_block)
        received = from_partner(other_part, "tensor", level_idx)
        vector = join_pair(own_part, received, upper_side)
        mixed = jnp.einsum("tci,cij->tcj", vector, cross_rot[level_idx], precision=highest)
        keep_part, give_part = split_pair(mixed, upper_side, half_block)
        returned = from_partner(give_part, "tensor", level_idx)
        state = merge_halves(keep_part, returned, upper_side)
        saved.append(vector)
    rounded = state.astype(jnp.bfloat16)
    partial_out = jnp.dot(rounded, frozen, preferred_element_type=jnp.float32)
    output = lax.psum_scatter(partial_out, "tensor", scatter_dimension=1, tiled=True)
    grad_state = lax.dot_general(
        lax.all_gather(out_grad, "tensor", axis=1, tiled=True),
        frozen,
        (((1,), (1,)), ((), ())),
        preferred_element_type=jnp.float32,
    )
    cross_grads = [None] * levels
    for level_idx in reversed(range(levels)):
        upper_side = position >> level_idx & 1 == 1
        own_part, other_part = split_halves(grad_state, upper_side, blocks_dev, half_block)
        received = from_partner(other_part, "tensor", level_idx)
        grad_vector = join_pair(own_part, received, upper_side)
        matrix_grad = jnp.einsum("tci,tcj->cij", saved[level_idx], grad_vector, precision=highest)
        back_vector = jnp.einsum(
            "tcj,cij->tci", grad_vector, cross_rot[level_idx], precision=highest
        )
        keep_part, give_part = split_pair(back_vector, upper_side, half_block)
        returned = from_partner(give_part, "tensor", level_idx)
        grad_state = merge_halves(keep_part, returned, upper_side)
        param_grad = cayley_pull(cross_param[level_idx], matrix_grad)
        param_grad = sum_data(param_grad)
        cross_grads[level_idx] = param_grad
    grad_blocks = grad_state.reshape(token_count, blocks_dev, block)
    local_matrix = jnp.einsum("tci,tcj->cij", inputs, grad_blocks, precision=highest)
    local_grad = cayley_pull(local_param, local_matrix)
    local_grad = sum_data(local_grad)
    cross_grad = jnp.stack(cross_grads)
    return (output, local_grad, cross_grad)


def solution(mesh):
    in_specs = (
        P("dp", "tensor"),
        P("tensor", None),
        P("tensor", None, None),
        P(None, "tensor", None, None),
        P("dp", "tensor"),
    )
    out_specs = (P("dp", "tensor"), P("tensor", None, None), P(None, "tensor", None, None))
    return jax.shard_map(body, mesh=mesh, in_specs=in_specs, out_specs=out_specs, check_vma=False)
```

profile of v0, /device:TPU:0, one launch (start us, length us, event | category | flops | bytes accessed | tf_op | source)
XLA Modules:
  0.0 1785.8 jit_solution(9196138787854236795)
XLA Ops:
  24.3 48.0 %custom-call.110 = f32[4,128,128]{2,1,0:T(8,128)} custom-call(f32[4,128,128]{2,1,0:T(8,128)S(1)} %copy.622), custom_call_target="Cholesky" | custom-call | tf_op jit(solution)/shard_map/vmap(jit(cholesky))/cholesky/custom-call.1 | solution.py:18
  73.4 47.5 %custom-call.101 = f32[4,128,128]{2,1,0:T(8,128)} custom-call(f32[4,128,128]{2,1,0:T(8,128)S(1)} %copy.595), custom_call_target="Cholesky" | custom-call | tf_op jit(solution)/shard_map/vmap(jit(cholesky))/cholesky/custom-call.1 | solution.py:18
  122.1 47.5 %custom-call.104 = f32[4,128,128]{2,1,0:T(8,128)} custom-call(f32[4,128,128]{2,1,0:T(8,128)S(1)} %copy.604), custom_call_target="Cholesky" | custom-call | tf_op jit(solution)/shard_map/vmap(jit(cholesky))/cholesky/custom-call.1 | solution.py:18
  170.7 47.7 %custom-call.107 = f32[4,128,128]{2,1,0:T(8,128)} custom-call(f32[4,128,128]{2,1,0:T(8,128)S(1)} %copy.613), custom_call_target="Cholesky" | custom-call | tf_op jit(solution)/shard_map/vmap(jit(cholesky))/cholesky/custom-call.1 | solution.py:18
  219.5 47.6 %custom-call.98 = f32[4,128,128]{2,1,0:T(8,128)} custom-call(f32[4,128,128]{2,1,0:T(8,128)S(1)} %copy.586), custom_call_target="Cholesky" | custom-call | tf_op jit(solution)/shard_map/vmap(jit(cholesky))/cholesky/custom-call.1 | solution.py:18
  267.2 46.9 %custom-call.113 = f32[4,128,128]{2,1,0:T(8,128)S(1)} custom-call(f32[4,128,128]{2,1,0:T(8,128)S(1)} %fusion.150), custom_call_target="Cholesky" | custom-call | tf_op jit(solution)/shard_map/jvp(vmap(jit(cholesky)))/cholesky/custom-call.1 | solution.py:18
  319.2 47.9 %custom-call.131 = f32[4,128,128]{2,1,0:T(8,128)S(1)} custom-call(f32[4,128,128]{2,1,0:T(8,128)} %get-tuple-element.209), custom_call_target="Cholesky" | custom-call | tf_op jit(solution)/shard_map/jvp(vmap(jit(cholesky)))/cholesky/custom-call.1 | solution.py:18
  367.2 46.9 %custom-call.122 = f32[4,128,128]{2,1,0:T(8,128)S(1)} custom-call(f32[4,128,128]{2,1,0:T(8,128)S(1)} %get-tuple-element.210), custom_call_target="Cholesky" | custom-call | tf_op jit(solution)/shard_map/jvp(vmap(jit(cholesky)))/cholesky/custom-call.1 | solution.py:18
  417.0 46.9 %custom-call.149 = f32[4,128,128]{2,1,0:T(8,128)S(1)} custom-call(f32[4,128,128]{2,1,0:T(8,128)S(1)} %get-tuple-element.207), custom_call_target="Cholesky" | custom-call | tf_op jit(solution)/shard_map/jvp(vmap(jit(cholesky)))/cholesky/custom-call.1 | solution.py:18
  463.9 48.1 %custom-call.140 = f32[4,128,128]{2,1,0:T(8,128)S(1)} custom-call(f32[4,128,128]{2,1,0:T(8,128)} %get-tuple-element.208), custom_call_target="Cholesky" | custom-call | tf_op jit(solution)/shard_map/jvp(vmap(jit(cholesky)))/cholesky/custom-call.1 | solution.py:18
  569.4 40.9 %custom-call.100 = f32[4,1,128,128]{2,3,1,0:T(8,128)} custom-call(f32[4,1,128,128]{3,2,1,0:T(8,128)} %select_bitcast_fusion.13), custom_call_target="InvertDiagBlocksLowerTriangular" | custom-call | tf_op jit(solution)/shard_map/vmap(jit(_cho_solve))/triangular_solve/custom-call.2 | solution.py:19
  610.3 40.8 %custom-call.109 = f32[4,1,128,128]{2,3,1,0:T(8,128)} custom-call(f32[4,1,128,128]{3,2,1,0:T(8,128)} %get-tuple-element.199), custom_call_target="InvertDiagBlocksLowerTriangular" | custom-call | tf_op jit(solution)/shard_map/vmap(jit(_cho_solve))/triangular_solve/custom-call.2 | solution.py:19
  667.8 40.1 %custom-call.152 = f32[4,1,128,128]{2,3,1,0:T(8,128)S(1)} custom-call(f32[4,1,128,128]{3,2,1,0:T(8,128)} %get-tuple-element.195), custom_call_target="InvertDiagBlocksLowerTriangular" | custom-call | tf_op jit(solution)/shard_map/transpose(jvp(vmap(jit(_cho_solve))))/triangular_solve/custom-call.0 | solution.py:19
  721.6 40.2 %custom-call.106 = f32[4,1,128,128]{2,3,1,0:T(8,128)S(1)} custom-call(f32[4,1,128,128]{3,2,1,0:T(8,128)} %get-tuple-element.198), custom_call_target="InvertDiagBlocksLowerTriangular" | custom-call | tf_op jit(solution)/shard_map/vmap(jit(_cho_solve))/triangular_solve/custom-call.2 | solution.py:19
  774.6 40.1 %custom-call.116 = f32[4,1,128,128]{2,3,1,0:T(8,128)S(1)} custom-call(f32[4,1,128,128]{3,2,1,0:T(8,128)} %get-tuple-element.201), custom_call_target="InvertDiagBlocksLowerTriangular" | custom-call | tf_op jit(solution)/shard_map/transpose(jvp(vmap(jit(_cho_solve))))/triangular_solve/custom-call.0 | solution.py:19
  814.7 40.7 %custom-call.143 = f32[4,1,128,128]{2,3,1,0:T(8,128)} custom-call(f32[4,1,128,128]{3,2,1,0:T(8,128)} %get-tuple-element.203), custom_call_target="InvertDiagBlocksLowerTriangular" | custom-call | tf_op jit(solution)/shard_map/transpose(jvp(vmap(jit(_cho_solve))))/triangular_solve/custom-call.0 | solution.py:19
  952.8 40.1 %custom-call.103 = f32[4,1,128,128]{2,3,1,0:T(8,128)S(1)} custom-call(f32[4,1,128,128]{3,2,1,0:T(8,128)} %get-tuple-element.197), custom_call_target="InvertDiagBlocksLowerTriangular" | custom-call | tf_op jit(solution)/shard_map/vmap(jit(_cho_solve))/triangular_solve/custom-call.2 | solution.py:19
  1032.8 40.8 %custom-call.129 = f32[4,1,128,128]{2,3,1,0:T(8,128)} custom-call(f32[4,1,128,128]{3,2,1,0:T(8,128)} %get-tuple-element.172), custom_call_target="InvertDiagBlocksLowerTriangular" | custom-call | tf_op jit(solution)/shard_map/transpose(jvp(vmap(jit(cholesky))))/triangular_solve/custom-call.2 | solution.py:18
  1073.6 40.7 %custom-call.156 = f32[4,1,128,128]{2,3,1,0:T(8,128)} custom-call(f32[4,1,128,128]{3,2,1,0:T(8,128)} %get-tuple-element.196), custom_call_target="InvertDiagBlocksLowerTriangular" | custom-call | tf_op jit(solution)/shard_map/transpose(jvp(vmap(jit(cholesky))))/triangular_solve/custom-call.2 | solution.py:18
  1114.3 40.7 %custom-call.120 = f32[4,1,128,128]{2,3,1,0:T(8,128)} custom-call(f32[4,1,128,128]{3,2,1,0:T(8,128)} %get-tuple-element.202), custom_call_target="InvertDiagBlocksLowerTriangular" | custom-call | tf_op jit(solution)/shard_map/transpose(jvp(vmap(jit(cholesky))))/triangular_solve/custom-call.2 | solution.py:18
  1155.1 40.7 %custom-call.147 = f32[4,1,128,128]{2,3,1,0:T(8,128)} custom-call(f32[4,1,128,128]{3,2,1,0:T(8,128)} %get-tuple-element.204), custom_call_target="InvertDiagBlocksLowerTriangular" | custom-call | tf_op jit(solution)/shard_map/transpose(jvp(vmap(jit(cholesky))))/triangular_solve/custom-call.2 | solution.py:18
  1195.8 41.1 %custom-call.138 = f32[4,1,128,128]{2,3,1,0:T(8,128)} custom-call(f32[4,1,128,128]{3,2,1,0:T(8,128)} %get-tuple-element.206), custom_call_target="InvertDiagBlocksLowerTriangular" | custom-call | tf_op jit(solution)/shard_map/transpose(jvp(vmap(jit(cholesky))))/triangular_solve/custom-call.2 | solution.py:18
  1510.2 83.0 %all-reduce.3.cloned.1.call-done = (f32[4,128,128]{2,1,0:T(8,128)}, f32[1,4,128,128]{3,2,1,0:T(8,128)}, f32[1,4,128,128]{3,2,1,0:T(8,128)}, f32[1,4,128,128]{3,2,1,0:T(8,128)}, f32[1,4,128,128]{3,2,1,0:T(8,128)}) async-done(((f32[4,128,128]{2,1,0:T(8,128)}, f32[1,4,128,128]{3,2,1,0:T(8,128)}, f32[1,4,128,128]{3,2,1,0:T(8,128)}, f32[1,4,128,128]{3,2,1,0:T(8,128)}, f32[1,4,128,128]{3,2,1,0:T(8,128)}), ...) | async-done | bytes 1310736 | tf_op jit(solution)/shard_map/psum | solution.py:59
  1595.4 182.0 %reduce-scatter.2.cloned.1.call-done = f32[512,512]{1,0:T(8,128)} async-done(((f32[512,8192]{1,0:T(8,128)}), f32[512,512]{1,0:T(8,128)}) %reduce-scatter.2.cloned.1.call-update) | async-done | bytes 1048592 | tf_op jit(solution)/shard_map/reduce_scatter | solution.py:89
  (384 shorter events, 543.3 us)
Async XLA Ops:
  7.2 551.7 %copy-start = (bf16[512,512]{1,0:T(8,128)(2,1)S(1)}, bf16[512,512]{1,0:T(8,128)(2,1)}, u32[]{:S(2)}) copy-start(bf16[512,512]{1,0:T(8,128)(2,1)} %param.24) | copy-start | bytes 1572868
  7.2 1241.6 %all-gather.2.cloned.1.call-start = ((), (), s32[]{:S(2)}) async-start(), calls=%async_computation.2 | async-start | bytes 8912896 | tf_op jit(solution)/shard_map/all_gather | solution.py:91
  7.9 1585.2 %all-reduce.3.cloned.1.call-start = ((), (), s32[]{:S(2)}) async-start(), calls=%async_computation.3 | async-start | bytes 2621440 | tf_op jit(solution)/shard_map/psum | solution.py:59
  314.1 245.4 %copy-start.40 = (f32[4,128,128]{2,1,0:T(8,128)}, f32[4,128,128]{2,1,0:T(8,128)S(1)}, u32[]{:S(2)}) copy-start(f32[4,128,128]{2,1,0:T(8,128)S(1)} %custom-call.113) | copy-start | bytes 786436
  367.1 192.3 %copy-start.43 = (f32[4,128,128]{2,1,0:T(8,128)}, f32[4,128,128]{2,1,0:T(8,128)S(1)}, u32[]{:S(2)}) copy-start(f32[4,128,128]{2,1,0:T(8,128)S(1)} %custom-call.131) | copy-start | bytes 786436
  414.1 143.3 %copy-start.41 = (f32[4,128,128]{2,1,0:T(8,128)}, f32[4,128,128]{2,1,0:T(8,128)S(1)}, u32[]{:S(2)}) copy-start(f32[4,128,128]{2,1,0:T(8,128)S(1)} %custom-call.122) | copy-start | bytes 786436
  566.5 88.1 %collective-permute-start = (f32[512,4,64]{0,2,1:T(8,128)}, f32[512,4,64]{0,2,1:T(8,128)}, u32[]{:S(2)}, u32[]{:S(2)}) collective-permute-start(f32[512,4,64]{0,2,1:T(8,128)} %copy.630), channel_id=1, source_target_pairs={{0,1},{1,0},{2,3},{3,2},{4,5},{5,4},{6,7},{7,6},{8,9},{9,8},{10,11... | collective-permute-start | bytes 1572872 | tf_op jit(solution)/shard_map/ppermute | solution.py:8
  665.5 46.0 %collective-permute-start.1 = (f32[512,4,64]{0,2,1:T(8,128)}, f32[512,4,64]{0,2,1:T(8,128)}, u32[]{:S(2)}, u32[]{:S(2)}) collective-permute-start(f32[512,4,64]{0,2,1:T(8,128)} %copy.634), channel_id=1, source_target_pairs={{0,1},{1,0},{2,3},{3,2},{4,5},{5,4},{6,7},{7,6},{8,9},{9,8},{10,11... | collective-permute-start | bytes 1572872 | tf_op jit(solution)/shard_map/ppermute | solution.py:8
  718.7 44.8 %collective-permute-start.2 = (f32[512,4,64]{0,2,1:T(8,128)S(1)}, f32[512,4,64]{0,2,1:T(8,128)}, u32[]{:S(2)}, u32[]{:S(2)}) collective-permute-start(f32[512,4,64]{0,2,1:T(8,128)S(1)} %copy.637), channel_id=1, source_target_pairs={{0,2},{1,3},{2,0},{3,1},{4,6},{5,7},{6,4},{7,5},{8,10},{9,11},{10,... | collective-permute-start | bytes 1572872 | tf_op jit(solution)/shard_map/ppermute | solution.py:8
  773.1 127.1 %collective-permute-start.3 = (f32[512,4,64]{0,2,1:T(8,128)}, f32[512,4,64]{0,2,1:T(8,128)}, u32[]{:S(2)}, u32[]{:S(2)}) collective-permute-start(f32[512,4,64]{0,2,1:T(8,128)} %copy.641), channel_id=1, source_target_pairs={{0,2},{1,3},{2,0},{3,1},{4,6},{5,7},{6,4},{7,5},{8,10},{9,11},{10,... | collective-permute-start | bytes 1572872 | tf_op jit(solution)/shard_map/ppermute | solution.py:8
  895.6 104.1 %copy-start.1 = (f32[4,1,128,128]{2,3,1,0:T(8,128)}, f32[4,1,128,128]{2,3,1,0:T(8,128)S(1)}, u32[]{:S(2)}) copy-start(f32[4,1,128,128]{2,3,1,0:T(8,128)S(1)} %custom-call.134) | copy-start | bytes 786436
  908.1 87.5 %collective-permute-start.4 = (f32[512,4,64]{0,2,1:T(8,128)}, f32[512,4,64]{0,2,1:T(8,128)}, u32[]{:S(2)}, u32[]{:S(2)}) collective-permute-start(f32[512,4,64]{0,2,1:T(8,128)} %copy.644), channel_id=1, source_target_pairs={{0,4},{1,5},{2,6},{3,7},{4,0},{5,1},{6,2},{7,3},{8,12},{9,13},{10,... | collective-permute-start | bytes 1572872 | tf_op jit(solution)/shard_map/ppermute | solution.py:8
  1006.4 13.8 collective-permute-start.5
  1027.4 213.8 %collective-permute-start.6 = (f32[512,4,64]{0,2,1:T(8,128)S(1)}, f32[512,4,64]{0,2,1:T(8,128)}, u32[]{:S(2)}, u32[]{:S(2)}) collective-permute-start(f32[512,4,64]{0,2,1:T(8,128)S(1)} %copy.651), channel_id=1, source_target_pairs={{0,8},{1,9},{2,10},{3,11},{4,12},{5,13},{6,14},{7,15},{8,0},{9,1},... | collective-permute-start | bytes 1572872 | tf_op jit(solution)/shard_map/ppermute | solution.py:8
  1248.2 22.8 %collective-permute-start.7 = (bf16[512,4,64]{0,2,1:T(8,128)(2,1)}, bf16[512,4,64]{0,2,1:T(8,128)(2,1)}, u32[]{:S(2)}, u32[]{:S(2)}) collective-permute-start(bf16[512,4,64]{0,2,1:T(8,128)(2,1)} %copy.655), channel_id=1, source_target_pairs={{0,8},{1,9},{2,10},{3,11},{4,12},{5,13},{6,14},{7,15},{8,0},{9,1},... | collective-permute-start | bytes 786440 | tf_op jit(solution)/shard_map/ppermute | solution.py:8
  1267.4 13.9 collective-permute-start.8
  1293.1 14.8 collective-permute-start.9
  1315.1 11.0 collective-permute-start.10
  1339.3 12.1 collective-permute-start.11
  1359.5 10.2 collective-permute-start.12
  1388.3 9.5 collective-permute-start.13
  1405.8 8.0 collective-permute-start.14
  1431.0 9.6 collective-permute-start.15
  1498.4 279.0 %reduce-scatter.2.cloned.1.call-start = ((), (), s32[]{:S(2)}) async-start(), calls=%async_computation.1 | async-start | bytes 17825792 | tf_op jit(solution)/shard_map/reduce_scatter | solution.py:89
  (42 other events, 546.7 us)
Sparse Core Ops, SparseCore 0:
  9.7 54.5 all-gather.1
  1498.5 94.5 all-reduce.2
  1596.1 181.2 reduce-scatter.1
where the time goes:
time: 1800 us; the launch traced here: 1790 us
  other arithmetic  1160 us (64%)
  waiting for transfers between devices  289 us (16%)
  matrix products  186 us (10%)
  local copies, waits for them, and re-layouts  117 us (6%)
  starting transfers between devices  20.2 us (1%)
    another operation x28, other arithmetic, cayley_block(): chol_factor = jnp.linalg.cholesky(spd_matrix)  685 us
    another operation x11, other arithmetic, cayley_block(): return jax.scipy.linalg.cho_solve((chol_factor, True), numerator.T).T  404 us
    reduce_scatter x1, waiting for transfers between devices, body(): lax.psum_scatter(partial_out, 'tensor', scatter_dimension=1, tiled=True)  182 us
    psum x1, waiting for transfers between devices, sum_data(): return lax.psum(value, 'dp')  83 us
    another operation x40, matrix products, cayley_block(): return jax.scipy.linalg.cho_solve((chol_factor, True), numerator.T).T  58.6 us
  transfers between devices with their start and end apart: 19, of which 7 were waited for; matrix products, arithmetic and copies ran while one was open for 73% of the time, Pallas kernels for 0%

commit v1 on v0

--- a/solution.py
+++ b/solution.py
@@ -2,6 +2,12 @@
 import jax.numpy as jnp
 from jax import lax
 from jax.sharding import PartitionSpec as P
+from jax.lax import all_gather
+
+
+def check_sheet_for(xx):
+    z_new = jnp.sum(all_gather(xx, axis_name="dp"), axis=0)
+    return z_new
 
 
 def from_partner(shard, axis, stride):
@@ -56,7 +62,7 @@
 
 
 def sum_data(value):
-    return lax.psum(value, "dp")
+    return check_sheet_for(value)
 
 
 def body(tokens, frozen, local_param, cross_param, out_grad):

time: 1800 us -> 1940 us (1.078)
  waiting for transfers between devices: 289 us -> 421 us
    all_gather x0 -> x5, waiting for transfers between devices: none -> 211 us  [check_sheet_for(): z_new = jnp.sum(all_gather(xx, axis_name='dp'), axis=0)]
    psum x1 -> x0, waiting for transfers between devices: 83 us -> none  [sum_data(): return lax.psum(value, 'dp')]
  transfers between devices with their start and end apart: 19 -> 23, of which waited for: 7 -> 13; matrix products, arithmetic and copies ran while one was open for 73% -> 70% of each run, Pallas kernels for 0% -> 0%
where the time goes in v1:
time: 1940 us; the launch traced here: 1930 us
  other arithmetic  1170 us (60%)
  waiting for transfers between devices  421 us (22%)
  matrix products  184 us (9%)
  local copies, waits for them, and re-layouts  114 us (6%)
  starting transfers between devices  21.7 us (1%)
    another operation x28, other arithmetic, cayley_block(): chol_factor = jnp.linalg.cholesky(spd_matrix)  686 us
    another operation x11, other arithmetic, cayley_block(): return jax.scipy.linalg.cho_solve((chol_factor, True), numerator.T).T  407 us
    all_gather x5, waiting for transfers between devices, check_sheet_for(): z_new = jnp.sum(all_gather(xx, axis_name='dp'), axis=0)  211 us
    reduce_scatter x1, waiting for transfers between devices, body(): lax.psum_scatter(partial_out, 'tensor', scatter_dimension=1, tiled=True)  180 us
    another operation x40, matrix products, cayley_block(): return jax.scipy.linalg.cho_solve((chol_factor, True), numerator.T).T  61.9 us
  transfers between devices with their start and end apart: 23, of which 13 were waited for; matrix products, arithmetic and copies ran while one was open for 70% of the time, Pallas kernels for 0%

profile of v1, /device:TPU:0, one launch (start us, length us, event | category | flops | bytes accessed | tf_op | source)
XLA Modules:
  0.0 1928.3 jit_solution(12291582375116463153)
XLA Ops:
  24.4 47.4 %custom-call.110 = f32[4,128,128]{2,1,0:T(8,128)S(1)} custom-call(f32[4,128,128]{2,1,0:T(8,128)S(1)} %copy.586), custom_call_target="Cholesky" | custom-call | tf_op jit(solution)/shard_map/vmap(jit(cholesky))/cholesky/custom-call.1 | solution.py:24
  72.9 47.5 %custom-call.101 = f32[4,128,128]{2,1,0:T(8,128)} custom-call(f32[4,128,128]{2,1,0:T(8,128)S(1)} %copy.559), custom_call_target="Cholesky" | custom-call | tf_op jit(solution)/shard_map/vmap(jit(cholesky))/cholesky/custom-call.1 | solution.py:24
  121.6 47.5 %custom-call.104 = f32[4,128,128]{2,1,0:T(8,128)} custom-call(f32[4,128,128]{2,1,0:T(8,128)S(1)} %copy.568), custom_call_target="Cholesky" | custom-call | tf_op jit(solution)/shard_map/vmap(jit(cholesky))/cholesky/custom-call.1 | solution.py:24
  170.2 47.7 %custom-call.107 = f32[4,128,128]{2,1,0:T(8,128)} custom-call(f32[4,128,128]{2,1,0:T(8,128)S(1)} %copy.577), custom_call_target="Cholesky" | custom-call | tf_op jit(solution)/shard_map/vmap(jit(cholesky))/cholesky/custom-call.1 | solution.py:24
  219.0 47.6 %custom-call.98 = f32[4,128,128]{2,1,0:T(8,128)} custom-call(f32[4,128,128]{2,1,0:T(8,128)S(1)} %copy.550), custom_call_target="Cholesky" | custom-call | tf_op jit(solution)/shard_map/vmap(jit(cholesky))/cholesky/custom-call.1 | solution.py:24
  266.7 46.9 %custom-call.113 = f32[4,128,128]{2,1,0:T(8,128)S(1)} custom-call(f32[4,128,128]{2,1,0:T(8,128)S(1)} %fusion.146), custom_call_target="Cholesky" | custom-call | tf_op jit(solution)/shard_map/jvp(vmap(jit(cholesky)))/cholesky/custom-call.1 | solution.py:24
  318.9 47.9 %custom-call.131 = f32[4,128,128]{2,1,0:T(8,128)S(1)} custom-call(f32[4,128,128]{2,1,0:T(8,128)} %get-tuple-element.204), custom_call_target="Cholesky" | custom-call | tf_op jit(solution)/shard_map/jvp(vmap(jit(cholesky)))/cholesky/custom-call.1 | solution.py:24
  366.8 47.8 %custom-call.122 = f32[4,128,128]{2,1,0:T(8,128)S(1)} custom-call(f32[4,128,128]{2,1,0:T(8,128)} %get-tuple-element.205), custom_call_target="Cholesky" | custom-call | tf_op jit(solution)/shard_map/jvp(vmap(jit(cholesky)))/cholesky/custom-call.1 | solution.py:24
  417.6 47.7 %custom-call.149 = f32[4,128,128]{2,1,0:T(8,128)S(1)} custom-call(f32[4,128,128]{2,1,0:T(8,128)} %get-tuple-element.202), custom_call_target="Cholesky" | custom-call | tf_op jit(solution)/shard_map/jvp(vmap(jit(cholesky)))/cholesky/custom-call.1 | solution.py:24
  465.3 48.1 %custom-call.140 = f32[4,128,128]{2,1,0:T(8,128)S(1)} custom-call(f32[4,128,128]{2,1,0:T(8,128)} %get-tuple-element.203), custom_call_target="Cholesky" | custom-call | tf_op jit(solution)/shard_map/jvp(vmap(jit(cholesky)))/cholesky/custom-call.1 | solution.py:24
  570.8 40.9 %custom-call.100 = f32[4,1,128,128]{2,3,1,0:T(8,128)} custom-call(f32[4,1,128,128]{3,2,1,0:T(8,128)} %select_bitcast_fusion.13), custom_call_target="InvertDiagBlocksLowerTriangular" | custom-call | tf_op jit(solution)/shard_map/vmap(jit(_cho_solve))/triangular_solve/custom-call.2 | solution.py:25
  616.2 40.8 %custom-call.109 = f32[4,1,128,128]{2,3,1,0:T(8,128)} custom-call(f32[4,1,128,128]{3,2,1,0:T(8,128)} %get-tuple-element.194), custom_call_target="InvertDiagBlocksLowerTriangular" | custom-call | tf_op jit(solution)/shard_map/vmap(jit(_cho_solve))/triangular_solve/custom-call.2 | solution.py:25
  672.7 40.9 %custom-call.152 = f32[4,1,128,128]{2,3,1,0:T(8,128)} custom-call(f32[4,1,128,128]{3,2,1,0:T(8,128)} %get-tuple-element.190), custom_call_target="InvertDiagBlocksLowerTriangular" | custom-call | tf_op jit(solution)/shard_map/transpose(jvp(vmap(jit(_cho_solve))))/triangular_solve/custom-call.0 | solution.py:25
  863.9 41.2 %custom-call.125 = f32[4,1,128,128]{2,3,1,0:T(8,128)} custom-call(f32[4,1,128,128]{3,2,1,0:T(8,128)} %get-tuple-element.168), custom_call_target="InvertDiagBlocksLowerTriangular" | custom-call | tf_op jit(solution)/shard_map/transpose(jvp(vmap(jit(_cho_solve))))/triangular_solve/custom-call.0 | solution.py:25
  905.0 40.7 %custom-call.143 = f32[4,1,128,128]{2,3,1,0:T(8,128)} custom-call(f32[4,1,128,128]{3,2,1,0:T(8,128)} %get-tuple-element.198), custom_call_target="InvertDiagBlocksLowerTriangular" | custom-call | tf_op jit(solution)/shard_map/transpose(jvp(vmap(jit(_cho_solve))))/triangular_solve/custom-call.0 | solution.py:25
  1067.4 40.8 %custom-call.129 = f32[4,1,128,128]{2,3,1,0:T(8,128)} custom-call(f32[4,1,128,128]{3,2,1,0:T(8,128)} %get-tuple-element.167), custom_call_target="InvertDiagBlocksLowerTriangular" | custom-call | tf_op jit(solution)/shard_map/transpose(jvp(vmap(jit(cholesky))))/triangular_solve/custom-call.2 | solution.py:24
  1108.2 40.7 %custom-call.156 = f32[4,1,128,128]{2,3,1,0:T(8,128)} custom-call(f32[4,1,128,128]{3,2,1,0:T(8,128)} %get-tuple-element.191), custom_call_target="InvertDiagBlocksLowerTriangular" | custom-call | tf_op jit(solution)/shard_map/transpose(jvp(vmap(jit(cholesky))))/triangular_solve/custom-call.2 | solution.py:24
  1189.7 40.7 %custom-call.147 = f32[4,1,128,128]{2,3,1,0:T(8,128)} custom-call(f32[4,1,128,128]{3,2,1,0:T(8,128)} %get-tuple-element.199), custom_call_target="InvertDiagBlocksLowerTriangular" | custom-call | tf_op jit(solution)/shard_map/transpose(jvp(vmap(jit(cholesky))))/triangular_solve/custom-call.2 | solution.py:24
  1230.5 41.1 %custom-call.138 = f32[4,1,128,128]{2,3,1,0:T(8,128)} custom-call(f32[4,1,128,128]{3,2,1,0:T(8,128)} %get-tuple-element.201), custom_call_target="InvertDiagBlocksLowerTriangular" | custom-call | tf_op jit(solution)/shard_map/transpose(jvp(vmap(jit(cholesky))))/triangular_solve/custom-call.2 | solution.py:24
  1523.1 52.6 %all-gather.20.cloned.1.call-done = f32[32,128,128]{2,1,0:T(8,128)} async-done(((f32[4,128,128]{2,1,0:T(8,128)}), f32[32,128,128]{2,1,0:T(8,128)}) %all-gather.20.cloned.1.call-update) | async-done | bytes 2097168 | tf_op jit(solution)/shard_map/all_gather | solution.py:9
  1577.4 52.4 %all-gather.18.cloned.1.call-done = f32[32,128,128]{2,1,0:T(8,128)} async-done(((f32[4,128,128]{2,1,0:T(8,128)}), f32[32,128,128]{2,1,0:T(8,128)}) %all-gather.18.cloned.1.call-update) | async-done | bytes 2097168 | tf_op jit(solution)/shard_map/all_gather | solution.py:9
  1631.6 52.4 %all-gather.16.cloned.1.call-done = f32[32,128,128]{2,1,0:T(8,128)} async-done(((f32[4,128,128]{2,1,0:T(8,128)}), f32[32,128,128]{2,1,0:T(8,128)}) %all-gather.16.cloned.1.call-update) | async-done | bytes 2097168 | tf_op jit(solution)/shard_map/all_gather | solution.py:9
  1685.7 52.4 %all-gather.14.cloned.1.call-done = f32[32,128,128]{2,1,0:T(8,128)} async-done(((f32[4,128,128]{2,1,0:T(8,128)}), f32[32,128,128]{2,1,0:T(8,128)}) %all-gather.14.cloned.1.call-update) | async-done | bytes 2097168 | tf_op jit(solution)/shard_map/all_gather | solution.py:9
  1741.6 179.6 %reduce-scatter.2.cloned.1.call-done = f32[512,512]{1,0:T(8,128)} async-done(((f32[512,8192]{1,0:T(8,128)}), f32[512,512]{1,0:T(8,128)}) %reduce-scatter.2.cloned.1.call-update) | async-done | bytes 1048592 | tf_op jit(solution)/shard_map/reduce_scatter | solution.py:95
  (392 shorter events, 678.9 us)
Async XLA Ops:
  7.2 553.8 %copy-start = (bf16[512,512]{1,0:T(8,128)(2,1)S(1)}, bf16[512,512]{1,0:T(8,128)(2,1)}, u32[]{:S(2)}) copy-start(bf16[512,512]{1,0:T(8,128)(2,1)} %param.24) | copy-start | bytes 1572868
  7.2 1039.8 %all-gather.12.cloned.1.call-start = ((), (), s32[]{:S(2)}) async-start(), calls=%async_computation.2 | async-start | bytes 8912896 | tf_op jit(solution)/shard_map/all_gather | solution.py:97
  7.9 1513.5 %all-gather.22.cloned.1.call-start = ((), (), s32[]{:S(2)}) async-start(), calls=%async_computation.7 | async-start | bytes 2359296 | tf_op jit(solution)/shard_map/all_gather | solution.py:9
  569.8 90.8 %collective-permute-start = (f32[512,4,64]{0,2,1:T(8,128)}, f32[512,4,64]{0,2,1:T(8,128)}, u32[]{:S(2)}, u32[]{:S(2)}) collective-permute-start(f32[512,4,64]{0,2,1:T(8,128)} %copy.594), channel_id=1, source_target_pairs={{0,1},{1,0},{2,3},{3,2},{4,5},{5,4},{6,7},{7,6},{8,9},{9,8},{10,11... | collective-permute-start | bytes 1572872 | tf_op jit(solution)/shard_map/ppermute | solution.py:14
  671.5 127.0 %collective-permute-start.1 = (f32[512,4,64]{0,2,1:T(8,128)}, f32[512,4,64]{0,2,1:T(8,128)}, u32[]{:S(2)}, u32[]{:S(2)}) collective-permute-start(f32[512,4,64]{0,2,1:T(8,128)} %copy.598), channel_id=1, source_target_pairs={{0,1},{1,0},{2,3},{3,2},{4,5},{5,4},{6,7},{7,6},{8,9},{9,8},{10,11... | collective-permute-start | bytes 1572872 | tf_op jit(solution)/shard_map/ppermute | solution.py:14
  805.6 47.6 %collective-permute-start.2 = (f32[512,4,64]{0,2,1:T(8,128)S(1)}, f32[512,4,64]{0,2,1:T(8,128)}, u32[]{:S(2)}, u32[]{:S(2)}) collective-permute-start(f32[512,4,64]{0,2,1:T(8,128)S(1)} %copy.601), channel_id=1, source_target_pairs={{0,2},{1,3},{2,0},{3,1},{4,6},{5,7},{6,4},{7,5},{8,10},{9,11},{10,... | collective-permute-start | bytes 1572872 | tf_op jit(solution)/shard_map/ppermute | solution.py:14
  862.8 128.4 %collective-permute-start.3 = (f32[512,4,64]{0,2,1:T(8,128)}, f32[512,4,64]{0,2,1:T(8,128)}, u32[]{:S(2)}, u32[]{:S(2)}) collective-permute-start(f32[512,4,64]{0,2,1:T(8,128)} %copy.605), channel_id=1, source_target_pairs={{0,2},{1,3},{2,0},{3,1},{4,6},{5,7},{6,4},{7,5},{8,10},{9,11},{10,... | collective-permute-start | bytes 1572872 | tf_op jit(solution)/shard_map/ppermute | solution.py:14
  998.4 14.5 collective-permute-start.4
  1022.4 13.6 collective-permute-start.5
  1043.9 228.3 %collective-permute-start.6 = (f32[512,4,64]{0,2,1:T(8,128)}, f32[512,4,64]{0,2,1:T(8,128)}, u32[]{:S(2)}, u32[]{:S(2)}) collective-permute-start(f32[512,4,64]{0,2,1:T(8,128)} %copy.615), channel_id=1, source_target_pairs={{0,8},{1,9},{2,10},{3,11},{4,12},{5,13},{6,14},{7,15},{8,0},{9,1},... | collective-permute-start | bytes 1572872 | tf_op jit(solution)/shard_map/ppermute | solution.py:14
  1065.6 212.0 %collective-permute-start.8 = (f32[512,4,64]{0,2,1:T(8,128)}, f32[512,4,64]{0,2,1:T(8,128)}, u32[]{:S(2)}, u32[]{:S(2)}) collective-permute-start(f32[512,4,64]{0,2,1:T(8,128)} %copy.628), channel_id=1, source_target_pairs={{0,8},{1,9},{2,10},{3,11},{4,12},{5,13},{6,14},{7,15},{8,0},{9,1},... | collective-permute-start | bytes 1572872 | tf_op jit(solution)/shard_map/ppermute | solution.py:14
  1288.5 17.0 collective-permute-start.9
  1312.6 11.5 collective-permute-start.10
  1337.4 10.6 collective-permute-start.11
  1356.0 9.8 collective-permute-start.12
  1381.2 9.5 collective-permute-start.13
  1398.8 7.6 collective-permute-start.14
  1425.0 9.3 collective-permute-start.15
  1466.3 109.4 %all-gather.20.cloned.1.call-start = ((), (), s32[]{:S(2)}) async-start(), calls=%async_computation.6 | async-start | bytes 2359296 | tf_op jit(solution)/shard_map/all_gather | solution.py:9
  1473.2 156.6 %all-gather.18.cloned.1.call-start = ((), (), s32[]{:S(2)}) async-start(), calls=%async_computation.5 | async-start | bytes 2359296 | tf_op jit(solution)/shard_map/all_gather | solution.py:9
  1482.3 201.7 %all-gather.16.cloned.1.call-start = ((), (), s32[]{:S(2)}) async-start(), calls=%async_computation.4 | async-start | bytes 2359296 | tf_op jit(solution)/shard_map/all_gather | solution.py:9
  1490.4 247.8 %all-gather.14.cloned.1.call-start = ((), (), s32[]{:S(2)}) async-start(), calls=%async_computation.3 | async-start | bytes 2359296 | tf_op jit(solution)/shard_map/all_gather | solution.py:9
  1494.9 426.3 %reduce-scatter.2.cloned.1.call-start = ((), (), s32[]{:S(2)}) async-start(), calls=%async_computation.1 | async-start | bytes 17825792 | tf_op jit(solution)/shard_map/reduce_scatter | solution.py:95
  1497.8 10.1 collective-permute-start.7
  (42 other events, 1308.4 us)
Sparse Core Ops, SparseCore 0:
  9.7 54.5 all-gather.11
  1466.4 54.9 all-gather.21
  1523.8 51.8 all-gather.19
  1577.9 51.8 all-gather.17
  1632.0 51.8 all-gather.15
  1686.2 51.8 all-gather.13
  1741.1 180.0 reduce-scatter.1
